TPU v7x, 256 devices: a whole 4x4x8 slice. The times are simulated.
256 devices in a mesh: pipe: 2 (over core), expert: 16 (over y, x), dp: 8 (over z).
Axes of the slice: x: 4, y: 4, z: 8, core: 2. Of those that a mesh axis runs over, the one named last changes fastest.
Arguments:
- tokens: bfloat16 [2048, 6144], P('expert'), may hold values from -6 to 6
- expert_ids: int32 [2048, 2], P('expert'), may hold values from 0 to 15, all different within a row; in each aligned block of 128 rows (0 to 127, 128 to 255, ...) at most 24 rows name the same one
- w_router: bfloat16 [6144, 16], replicated, may hold values from -0.078125 to 0.078125
- w_gate: bfloat16 [16, 6144, 4096], P('expert', None, ('pipe', 'dp')), may hold values from -0.078125 to 0.078125
- w_up: bfloat16 [16, 6144, 4096], P('expert', None, ('pipe', 'dp')), may hold values from -0.078125 to 0.078125
- w_down: bfloat16 [16, 4096, 6144], P('expert', ('pipe', 'dp')), may hold values from -0.125 to 0.125
Outputs:
- mixed: bfloat16 [2048, 6144], P('expert', ('pipe', 'dp'))
Inputs may be any that keep to these rules, and one draw needn't show every extreme that they name: `expert_ids`: in each aligned block of 128 tokens no expert is named by more than 24 of the block's choices, a bound that some block reaches; the two experts of a token differ.
All inputs are finite; a program needn't handle non-finite values.
Results may differ from a plain program's by a relative error of at most 0.018.
Values may be sent and summed in bfloat16 or wider, within the bound.
A program may use at most 64 MiB of HBM per device.

v0:
```python
import jax
import jax.numpy as jnp
from jax import lax
from jax.sharding import PartitionSpec as P


def slots_of(ids, experts):
    blocks = ids.shape[0]
    flat = ids.reshape(blocks, -1)
    onehot = (flat[:, :, None] == jnp.arange(experts, dtype=jnp.int32)[None, None, :]).astype(
        jnp.int32
    )
    before = jnp.cumsum(onehot, axis=1) - onehot
    slot = jnp.sum(before * onehot, axis=-1)
    return (flat, slot)


def dispatch(x_rows, id_rows, experts, capacity):
    count, width = x_rows.shape
    topk = id_rows.shape[1]
    flat, slot = slots_of(id_rows[None], experts)
    dest = flat[0] * capacity + slot[0]
    select = (jnp.arange(experts * capacity, dtype=jnp.int32)[:, None] == dest[None, :]).astype(
        jnp.bfloat16
    )
    repeated = jnp.repeat(x_rows, topk, axis=0)
    placed = jnp.dot(select, repeated, preferred_element_type=jnp.float32).astype(jnp.bfloat16)
    return (placed.reshape(experts, capacity, width), dest)


def body(tokens, expert_ids, w_router, w_gate, w_up, w_down):
    count, width = tokens.shape
    topk = expert_ids.shape[1]
    experts = lax.axis_size("expert") * w_gate.shape[0]
    capacity = 3 * count * topk // (2 * experts)
    groups = lax.axis_size(("pipe", "dp"))
    columns = width // groups
    start = lax.axis_index(("pipe", "dp")) * columns
    mine = lax.dynamic_slice_in_dim(tokens, start, columns, 1)
    local, dest = dispatch(mine, expert_ids, experts, capacity)
    arrived = lax.all_to_all(local, "expert", split_axis=0, concat_axis=0, tiled=True)
    arrived = arrived.reshape(experts * capacity, columns)
    inputs = lax.all_gather(arrived, ("pipe", "dp"), axis=1, tiled=True)
    gate = jnp.dot(inputs, w_gate[0], preferred_element_type=jnp.float32)
    upper = jnp.dot(inputs, w_up[0], preferred_element_type=jnp.float32)
    hidden = (jax.nn.silu(gate) * upper).astype(jnp.bfloat16)
    term = jnp.dot(hidden, w_down[0], preferred_element_type=jnp.float32).astype(jnp.bfloat16)
    logits = jnp.dot(tokens, w_router, preferred_element_type=jnp.float32)
    chosen = jnp.take_along_axis(logits, expert_ids, axis=1)
    first = jax.nn.sigmoid(chosen[:, 0] - chosen[:, 1])
    gates = jnp.stack([first, 1.0 - first], axis=1)
    summed = lax.psum_scatter(term, ("pipe", "dp"), scatter_dimension=1, tiled=True)
    returned = lax.all_to_all(
        summed.reshape(experts, capacity, columns),
        "expert",
        split_axis=0,
        concat_axis=0,
        tiled=True,
    )
    picked = jnp.take(returned.reshape(experts * capacity, columns), dest, axis=0)
    picked = picked.reshape(count, topk, columns).astype(jnp.float32)
    return jnp.sum(gates[:, :, None] * picked, axis=1).astype(jnp.bfloat16)


def solution(mesh):
    placed = (
        P("expert", None),
        P("expert", None),
        P(),
        P("expert", None, ("pipe", "dp")),
        P("expert", None, ("pipe", "dp")),
        P("expert", ("pipe", "dp"), None),
    )
    return jax.shard_map(
        body, mesh=mesh, in_specs=placed, out_specs=P("expert", ("pipe", "dp")), check_vma=False
    )
```

profile of v0, /device:TPU:1, one launch (start us, length us, event | category | flops | bytes accessed | tf_op | source)
XLA Modules:
  0.0 195.6 jit_solution(6473342927977986380)
XLA Ops:
  6.5 0.0 copy-start
  6.5 0.0 all-gather.2.cloned.1.call-start
  6.5 0.9 copy.45
  7.5 0.1 eq.40
  7.6 0.0 copy-start.5
  7.7 0.6 reduce-window.6
  8.2 0.8 slice_reduce_fusion
  9.0 0.0 copy-done.5
  9.0 0.9 constant_dynamic-slice_fusion
  9.9 0.1 broadcast_in_dim.23
  10.1 0.1 reshape.198
  10.1 0.7 reduce-window.9
  10.9 0.1 copy.48
  10.9 0.1 broadcast.109
  11.0 0.7 fusion.20
  11.8 0.0 copy-start.3
  11.8 0.6 copy-done.3
  12.3 0.7 multiply_add_fusion
  13.0 0.3 convolution_convert_fusion.1
  13.3 15.7 %all_to_all.10 = bf16[16,24,384]{2,1,0:T(8,128)(2,1)} all-to-all(bf16[16,24,384]{2,1,0:T(8,128)(2,1)S(1)} %bitcast.50), channel_id=1, replica_groups=mesh['pipe'=2,'expert'=16,'dp'=8] {'expert'}, dimensions={0} | all-to-all | bytes 589824 | tf_op jit(solution)/shard_map/all_to_all | solution.py:41
  28.9 0.0 all-gather.2.cloned.1.call-update
  29.0 0.0 reduce-scatter.4.cloned.1.call-start
  29.0 43.7 %all-gather.2.cloned.1.call-done = bf16[384,6144]{1,0:T(8,128)(2,1)} async-done(((bf16[384,384]{1,0:T(8,128)(2,1)}), bf16[384,6144]{1,0:T(8,128)(2,1)}) %all-gather.2.cloned.1.call-update) | async-done | bytes 4718608 | tf_op jit(solution)/shard_map/all_gather | solution.py:43
  72.8 4.7 %fusion.3 = f32[384,256]{1,0:T(8,128)S(1)} fusion(bf16[384,6144]{1,0:T(8,128)(2,1)} %all-gather.2.cloned.1.call-done, bf16[1,6144,256]{2,1,0:T(8,128)(2,1)} %param.9), kind=kOutput, calls=%fused_computation.6 | convolution fusion | flops 1207959552 | bytes 8257536 | tf_op jit(solution)/shard_map/dot_general | solution.py:44
  77.5 0.0 copy-done
  77.5 10.6 %convolution_convert_fusion = bf16[384,6144]{1,0:T(8,128)(2,1)} fusion(bf16[1,256,6144]{2,1,0:T(8,128)(2,1)S(1)} %copy-done, bf16[384,6144]{1,0:T(8,128)(2,1)} %all-gather.2.cloned.1.call-done, bf16[1,6144,256]{2,1,0:T(8,128)(2,1)} %param.10, f32[384,256]{1,0:T(8,128)S(1)} %fusion.3), kind=kOutput, calls=%fused_computation.2 | convolution fusion | flops 2418868224 | bytes 16121856 | tf_op jit(solution)/shard_map/dot_general | solution.py:47
  88.0 6.6 %copy.52 = bf16[384,6144]{0,1:T(8,128)(2,1)} copy(bf16[384,6144]{1,0:T(8,128)(2,1)} %convolution_convert_fusion) | data formatting | bytes 9437184
  94.7 0.0 copy-start.4
  94.7 0.0 copy-start.2
  94.7 0.0 copy-start.1
  94.7 0.0 reduce-scatter.4.cloned.1.call-update
  94.7 0.6 copy-done.4
  95.3 0.1 reduce_sum.23
  95.5 0.0 copy-done.2
  95.5 0.1 copy.51
  95.6 0.1 mul.61
  95.7 0.1 copy.49
  95.8 0.1 copy.50
  96.0 0.1 copy.42
  96.1 0.1 reshape.211
  96.3 0.0 copy-done.1
  96.3 1.9 fusion.22
  98.2 2.0 %gather_fusion.1 = f32[256]{0:T(256)S(1)} fusion(f32[128,16]{0,1:T(8,128)S(1)} %fusion.22, s32[256]{0:T(256)S(1)} %reshape.211), kind=kCustom, calls=%fused_computation.1 | custom fusion | bytes 4096 | tf_op jit(solution)/shard_map/jit(take_along_axis)/gather | solution.py:49
  100.2 0.1 reshape.214
  100.3 0.1 copy.43
  100.4 0.1 copy.44
  100.5 67.4 %reduce-scatter.4.cloned.1.call-done = bf16[384,384]{1,0:T(8,128)(2,1)} async-done(((bf16[6144,384]{1,0:T(8,128)(2,1)}), bf16[384,384]{1,0:T(8,128)(2,1)}) %reduce-scatter.4.cloned.1.call-update) | async-done | bytes 294928
  168.0 1.8 copy.53
  169.8 6.3 %all-to-all-start.1 = ((bf16[16,24,384]{2,1,0:T(8,128)(2,1)}), bf16[16,24,384]{2,1,0:T(8,128)(2,1)S(1)}, u32[]{:S(2)}, u32[]{:S(2)}) async-start(bf16[16,24,384]{2,1,0:T(8,128)(2,1)} %bitcast.49), calls=%async_computation.1 | async-start | bytes 589824 | tf_op jit(solution)/shard_map/all_to_all | solution.py:53
  176.2 8.5 %all-to-all-done.1 = bf16[16,24,384]{2,1,0:T(8,128)(2,1)S(1)} async-done(((bf16[16,24,384]{2,1,0:T(8,128)(2,1)}), bf16[16,24,384]{2,1,0:T(8,128)(2,1)S(1)}, u32[]{:S(2)}, u32[]{:S(2)}) %all-to-all-start.1) | async-done | bytes 294944 | tf_op jit(solution)/shard_map/all_to_all | solution.py:53
  184.6 1.8 gather_fusion
  186.5 1.0 gather.12
  187.5 1.3 multiply_reduce_fusion
  (12 shorter events, 0.1 us)
Async XLA Ops:
  6.5 70.9 %copy-start = (bf16[1,256,6144]{2,1,0:T(8,128)(2,1)S(1)}, bf16[1,256,6144]{2,1,0:T(8,128)(2,1)}, u32[]{:S(2)}) copy-start(bf16[1,256,6144]{2,1,0:T(8,128)(2,1)} %param.11) | copy-start | bytes 9437188
  6.5 66.2 %all-gather.2.cloned.1.call-start = ((), (), s32[]{:S(2)}) async-start(), calls=%async_computation.3 | async-start | bytes 5013504 | tf_op jit(solution)/shard_map/all_gather | solution.py:43
  7.6 1.4 copy-start.5
  11.8 0.6 copy-start.3
  29.0 139.0 %reduce-scatter.4.cloned.1.call-start = ((), (), s32[]{:S(2)}) async-start(), calls=%async_computation.4 | async-start | bytes 5013504
  94.7 0.7 copy-start.4
  94.7 0.8 copy-start.2
  94.7 1.6 copy-start.1
  169.8 14.8 %all-to-all-start.1 = ((bf16[16,24,384]{2,1,0:T(8,128)(2,1)}), bf16[16,24,384]{2,1,0:T(8,128)(2,1)S(1)}, u32[]{:S(2)}, u32[]{:S(2)}) async-start(bf16[16,24,384]{2,1,0:T(8,128)(2,1)} %bitcast.49), calls=%async_computation.1 | async-start | bytes 589824 | tf_op jit(solution)/shard_map/all_to_all | solution.py:53
Sparse Core Ops, SparseCore 0:
  29.1 43.6 all-gather.1
  94.8 73.1 reduce-scatter.3
where the time goes:
time: 196 us
  waiting for transfers between devices  120 us (61%)
  local copies, waits for them, and re-layouts  18.7 us (10%)
  matrix products  17.4 us (9%)
  blocking collectives  15.7 us (8%)
  between operations  13.6 us (7%)
  starting transfers between devices  6.36 us (3%)
  other arithmetic  4.13 us (2%)
    unnamed x3, waiting for transfers between devices  67.5 us
    all_gather x1, waiting for transfers between devices, body(): inputs = lax.all_gather(arrived, ('pipe', 'dp'), axis=1, tiled=True)  43.7 us
    all_to_all x1, blocking collectives, body(): lax.all_to_all(local, 'expert', split_axis=0, concat_axis=0, tiled=True)  15.7 us
    unnamed x15, local copies, waits for them, and re-layouts  10.6 us
    dot_general x1, matrix products, body(): jnp.dot(hidden, w_down[0], preferred_element_type=jnp.float32)  10.6 us
    all_to_all x1, waiting for transfers between devices, body(): lax.all_to_all(summed.reshape(experts, capacity, columns), 'expert', spli...  8.47 us
    all_to_all x1, starting transfers between devices, body(): lax.all_to_all(summed.reshape(experts, capacity, columns), 'expert', spli...  6.32 us
    dot_general x1, matrix products, body(): gate = jnp.dot(inputs, w_gate[0], preferred_element_type=jnp.float32)  4.71 us
  transfers between devices with their start and end apart: 3, of which 3 were waited for; matrix products, arithmetic and copies ran while one was open for 3% of the time, Pallas kernels for 0%

commit v1 on v0

--- a/solution.py
+++ b/solution.py
@@ -40,7 +40,10 @@
     local, dest = dispatch(mine, expert_ids, experts, capacity)
     arrived = lax.all_to_all(local, "expert", split_axis=0, concat_axis=0, tiled=True)
     arrived = arrived.reshape(experts * capacity, columns)
-    inputs = lax.all_gather(arrived, ("pipe", "dp"), axis=1, tiled=True)
+    inputs = jnp.concatenate(
+        lax.all_to_all(jnp.stack([arrived] * lax.axis_size(("pipe", "dp"))), ("pipe", "dp"), 0, 0),
+        axis=1,
+    )
     gate = jnp.dot(inputs, w_gate[0], preferred_element_type=jnp.float32)
     upper = jnp.dot(inputs, w_up[0], preferred_element_type=jnp.float32)
     hidden = (jax.nn.silu(gate) * upper).astype(jnp.bfloat16)

time: 196 us -> 258 us (1.32)
  blocking collectives: 15.7 us -> 130 us
  waiting for transfers between devices: 120 us -> 72.9 us
  matrix products: 17.4 us -> 8.62 us
    all_to_all x0 -> x1, blocking collectives: none -> 115 us  [body(): lax.all_to_all(jnp.stack([arrived] * lax.axis_size(('pipe', 'dp'))), ('pi...]
    all_gather x1 -> x0, waiting for transfers between devices: 43.7 us -> none  [body(): inputs = lax.all_gather(arrived, ('pipe', 'dp'), axis=1, tiled=True)]
    dot_general x1, matrix products: 10.6 us -> 3.59 us  [body(): jnp.dot(hidden, w_down[0], preferred_element_type=jnp.float32)]
    dot_general x1, matrix products: 4.71 us -> 1.42 us  [body(): gate = jnp.dot(inputs, w_gate[0], preferred_element_type=jnp.float32)]
    unnamed x3 -> x2, waiting for transfers between devices: 67.5 us -> 64.7 us
    unnamed x15 -> x19, local copies, waits for them, and re-layouts: 10.6 us -> 11.1 us
  transfers between devices with their start and end apart: 3 -> 2, of which waited for: 3 -> 2; matrix products, arithmetic and copies ran while one was open for 3% -> 2% of each run, Pallas kernels for 0% -> 0%
where the time goes in v1:
time: 258 us; the launch traced here: 257 us
  blocking collectives  130 us (50%)
  waiting for transfers between devices  72.9 us (28%)
  local copies, waits for them, and re-layouts  21 us (8%)
  between operations  13.6 us (5%)
  matrix products  8.62 us (3%)
  starting transfers between devices  6.44 us (2%)
  other arithmetic  4.13 us (2%)
    all_to_all x1, blocking collectives, body(): lax.all_to_all(jnp.stack([arrived] * lax.axis_size(('pipe', 'dp'))), ('pi...  115 us
    unnamed x2, waiting for transfers between devices  64.7 us
    all_to_all x1, blocking collectives, body(): lax.all_to_all(local, 'expert', split_axis=0, concat_axis=0, tiled=True)  15.7 us
    unnamed x19, local copies, waits for them, and re-layouts  11.1 us
    all_to_all x1, waiting for transfers between devices, body(): lax.all_to_all(summed.reshape(experts, capacity, columns), 'expert', spli...  8.2 us
    all_to_all x1, starting transfers between devices, body(): lax.all_to_all(summed.reshape(experts, capacity, columns), 'expert', spli...  6.44 us
  transfers between devices with their start and end apart: 2, of which 2 were waited for; matrix products, arithmetic and copies ran while one was open for 2% of the time, Pallas kernels for 0%

profile of v1, /device:TPU:1, one launch (start us, length us, event | category | flops | bytes accessed | tf_op | source)
XLA Modules:
  0.0 257.0 jit_solution(4475885248191338239)
XLA Ops:
  6.5 0.0 copy-start
  6.5 0.0 reduce-scatter.4.cloned.1.call-start
  6.5 0.9 copy.48
  7.5 0.1 eq.40
  7.6 0.0 copy-start.7
  7.7 0.6 reduce-window.6
  8.2 0.8 slice_reduce_fusion
  9.0 0.0 copy-done.7
  9.0 0.9 constant_dynamic-slice_fusion
  9.9 0.1 broadcast_in_dim.23
  10.1 0.1 reshape.203
  10.1 0.7 reduce-window.9
  10.9 0.1 copy.51
  10.9 0.1 broadcast.110
  11.0 0.7 fusion.12
  11.8 0.0 copy-start.5
  11.8 0.6 copy-done.5
  12.3 0.7 multiply_add_fusion
  13.0 0.3 convolution_convert_fusion.1
  13.3 15.7 %all_to_all.15 = bf16[16,24,384]{2,1,0:T(8,128)(2,1)} all-to-all(bf16[16,24,384]{2,1,0:T(8,128)(2,1)S(1)} %bitcast.54), channel_id=1, replica_groups=mesh['pipe'=2,'expert'=16,'dp'=8] {'expert'}, dimensions={0} | all-to-all | bytes 589824 | tf_op jit(solution)/shard_map/all_to_all | solution.py:41
  28.9 1.2 copy.54
  30.1 0.6 stack.9
  30.7 0.0 copy-start.1
  30.7 114.7 %all_to_all.16 = bf16[16,384,384]{1,2,0:T(8,128)(2,1)S(1)} all-to-all(bf16[16,384,384]{1,2,0:T(8,128)(2,1)S(1)} %stack.9), channel_id=1, replica_groups=mesh['pipe'=2,'expert'=16,'dp'=8] {'pipe','dp'}, dimensions={0} | all-to-all | bytes 9437184 | tf_op jit(solution)/shard_map/all_to_all | solution.py:44
  145.4 0.0 copy-done.1
  145.4 0.0 copy-start.2
  145.4 1.4 fusion.3
  146.8 0.5 copy-done.2
  147.3 1.4 fusion.8
  148.7 0.0 copy-done
  148.7 3.6 %convolution_convert_fusion = bf16[384,6144]{1,0:T(8,128)(2,1)} fusion(bf16[384,256]{1,0:T(8,128)(2,1)S(1)} %fusion.8, bf16[1,256,6144]{2,1,0:T(8,128)(2,1)S(1)} %copy-done), kind=kOutput, calls=%fused_computation.2 | convolution fusion | flops 1210318848 | bytes 8060928 | tf_op jit(solution)/shard_map/dot_general | solution.py:50
  152.3 6.6 %copy.56 = bf16[384,6144]{0,1:T(8,128)(2,1)} copy(bf16[384,6144]{1,0:T(8,128)(2,1)} %convolution_convert_fusion) | data formatting | bytes 9437184
  159.0 0.0 copy-start.6
  159.0 0.0 copy-start.4
  159.0 0.0 copy-start.3
  159.0 0.0 reduce-scatter.4.cloned.1.call-update
  159.0 0.6 copy-done.6
  159.6 0.1 reduce_sum.23
  159.8 0.0 copy-done.4
  159.8 0.1 copy.55
  159.9 0.1 mul.61
  160.0 0.1 copy.52
  160.1 0.1 copy.53
  160.3 0.1 copy.45
  160.4 0.1 reshape.217
  160.6 0.0 copy-done.3
  160.6 1.9 fusion.13
  162.5 2.0 gather_fusion.1
  164.5 0.1 reshape.220
  164.6 0.1 copy.46
  164.7 0.1 copy.47
  164.8 64.7 %reduce-scatter.4.cloned.1.call-done = bf16[384,384]{1,0:T(8,128)(2,1)} async-done(((bf16[6144,384]{1,0:T(8,128)(2,1)}), bf16[384,384]{1,0:T(8,128)(2,1)}) %reduce-scatter.4.cloned.1.call-update) | async-done | bytes 294928
  229.5 1.8 copy.57
  231.4 6.4 %all-to-all-start.2 = ((bf16[16,24,384]{2,1,0:T(8,128)(2,1)}), bf16[16,24,384]{2,1,0:T(8,128)(2,1)S(1)}, u32[]{:S(2)}, u32[]{:S(2)}) async-start(bf16[16,24,384]{2,1,0:T(8,128)(2,1)} %bitcast.52), calls=%async_computation.2 | async-start | bytes 589824 | tf_op jit(solution)/shard_map/all_to_all | solution.py:56
  237.9 8.2 %all-to-all-done.2 = bf16[16,24,384]{2,1,0:T(8,128)(2,1)S(1)} async-done(((bf16[16,24,384]{2,1,0:T(8,128)(2,1)}), bf16[16,24,384]{2,1,0:T(8,128)(2,1)S(1)}, u32[]{:S(2)}, u32[]{:S(2)}) %all-to-all-start.2) | async-done | bytes 294944 | tf_op jit(solution)/shard_map/all_to_all | solution.py:56
  246.1 1.8 gather_fusion
  247.9 1.0 gather.12
  248.9 1.3 multiply_reduce_fusion
  (12 shorter events, 0.1 us)
Async XLA Ops:
  6.5 142.2 %copy-start = (bf16[1,256,6144]{2,1,0:T(8,128)(2,1)S(1)}, bf16[1,256,6144]{2,1,0:T(8,128)(2,1)}, u32[]{:S(2)}) copy-start(bf16[1,256,6144]{2,1,0:T(8,128)(2,1)} %param.11) | copy-start | bytes 9437188
  6.5 223.0 %reduce-scatter.4.cloned.1.call-start = ((), (), s32[]{:S(2)}) async-start(), calls=%async_computation.4 | async-start | bytes 5013504
  7.6 1.4 copy-start.7
  11.8 0.6 copy-start.5
  30.7 114.7 %copy-start.1 = (bf16[1,6144,256]{2,1,0:T(8,128)(2,1)S(1)}, bf16[1,6144,256]{2,1,0:T(8,128)(2,1)}, u32[]{:S(2)}) copy-start(bf16[1,6144,256]{2,1,0:T(8,128)(2,1)} %param.9) | copy-start | bytes 9437188
  145.4 1.9 copy-start.2
  159.0 0.7 copy-start.6
  159.0 0.8 copy-start.4
  159.0 1.6 copy-start.3
  231.4 14.7 %all-to-all-start.2 = ((bf16[16,24,384]{2,1,0:T(8,128)(2,1)}), bf16[16,24,384]{2,1,0:T(8,128)(2,1)S(1)}, u32[]{:S(2)}, u32[]{:S(2)}) async-start(bf16[16,24,384]{2,1,0:T(8,128)(2,1)} %bitcast.52), calls=%async_computation.2 | async-start | bytes 589824 | tf_op jit(solution)/shard_map/all_to_all | solution.py:56
Sparse Core Ops, SparseCore 0:
  159.1 70.3 reduce-scatter.3
